TPU v7x, 32 devices: a whole 2x2x4 slice. The times are simulated.
32 devices in a mesh: gx: 4 (over y, core), gy: 8 (over z, x).
Axes of the slice: x: 2, y: 2, z: 4, core: 2. Of those that a mesh axis runs over, the one named last changes fastest.
Arguments:
- a_rows: bfloat16 [196608, 1024], P(('gx', 'gy')), may hold values from -6 to 6
- heights: int32 [32], P('gx'), may hold values from 1 to 38, as said below
- destination: int32 [32, 48], P('gx'), may hold values from 0 to 1023, as said below
Outputs:
- ortho_rows: bfloat16 [131072, 1024], P(('gx', 'gy'))
- factor_r: float32 [1024, 1024], replicated
Inputs may be any that keep to these rules, and one draw needn't show every extreme that they name: Tiles 0 to heights[d] - 1 of device d are live, the others carry nothing of the problem; the largest value is reached in every draw. For a live tile, destination // 32 is a device with the same gx index as the tile's device; live tiles name distinct slots; one device sends at most one live tile to any other device; entries of tiles that are not live are meaningless.
All inputs are finite; a program needn't handle non-finite values.
Results may differ from a plain program's by a relative error of at most 0.00055.
Values may be sent and summed in bfloat16 or wider, within the bound.
A program may use at most 256 MiB of HBM per device.

v0:
```python
import math
import jax
import jax.numpy as jnp
from jax import lax
from jax.sharding import PartitionSpec as P

TILE = 128
SLOTS = 32


def factor(row_block):
    gram_local = lax.dot_general(
        row_block, row_block, (((0,), (0,)), ((), ())), preferred_element_type=jnp.float32
    )
    summed = lax.psum(gram_local, ("gx", "gy"))
    return jnp.linalg.cholesky(summed)


def normalise(low_factor, row_block, root_scale):
    solved = jax.scipy.linalg.solve_triangular(
        low_factor, row_block.astype(jnp.float32).T, lower=True
    )
    return (solved.T * root_scale).astype(jnp.bfloat16)


def on_device(a_rows, heights, destination):
    breadth = a_rows.shape[1]
    size_gy = lax.axis_size("gy")
    devices = lax.axis_size("gx") * size_gy
    group_pos = lax.axis_index("gy")
    my_index = lax.axis_index("gx") * size_gy + group_pos
    group_base = my_index - group_pos
    tile_stack = a_rows.reshape(-1, TILE, breadth)
    stored = tile_stack.shape[0]
    tile_ids = jnp.arange(stored, dtype=jnp.int32)
    peer_ids = jnp.arange(size_gy, dtype=jnp.int32)
    slot_ids = jnp.arange(SLOTS, dtype=jnp.int32)
    tile_live = tile_ids[None, :] < heights[:, None]
    target_dev = destination // SLOTS
    target_slot = destination % SLOTS
    own_live = tile_live[group_pos]
    own_dev = target_dev[group_pos]
    own_slot = target_slot[group_pos]
    leaving = own_live & (own_dev != my_index)
    chosen = leaving[None, :] & (own_dev[None, :] - group_base == peer_ids[:, None])
    send_index = jnp.sum(jnp.where(chosen, tile_ids[None, :], 0), axis=1)
    send_has = jnp.any(chosen, axis=1)
    arriving = tile_live & (target_dev == my_index) & (peer_ids[:, None] != group_pos)
    arrive_slot = jnp.sum(jnp.where(arriving, target_slot, 0), axis=1)
    arrive_has = jnp.any(arriving, axis=1)
    staying = own_live & (own_dev == my_index)
    own_match = staying[None, :] & (own_slot[None, :] == slot_ids[:, None])
    in_match = arrive_has[None, :] & (arrive_slot[None, :] == slot_ids[:, None])
    matched = jnp.concatenate([own_match, in_match], axis=1)
    source = jnp.sum(
        jnp.where(matched, jnp.arange(stored + size_gy, dtype=jnp.int32)[None, :], 0), axis=1
    )
    filled = jnp.any(matched, axis=1)
    root_scale = math.sqrt(devices * SLOTS * TILE)
    received = lax.all_to_all(
        jnp.where(send_has[:, None, None], tile_stack[send_index], jnp.zeros((), tile_stack.dtype)),
        "gy",
        split_axis=0,
        concat_axis=0,
        tiled=True,
    )
    combined = jnp.concatenate([tile_stack, received], axis=0)
    balanced = jnp.where(
        filled[:, None, None], combined[source], jnp.zeros((), tile_stack.dtype)
    ).reshape(-1, breadth)
    low_factor = factor(balanced)
    ortho_rows = normalise(low_factor, balanced, root_scale)
    return (ortho_rows, low_factor.T / root_scale)


def solution(mesh):
    placed = (P(("gx", "gy"), None), P("gx"), P("gx", None))
    return jax.shard_map(
        on_device,
        mesh=mesh,
        in_specs=placed,
        out_specs=(P(("gx", "gy"), None), P()),
        check_vma=False,
    )
```

profile of v0, /device:TPU:0, one launch (start us, length us, event | category | flops | bytes accessed | tf_op | source)
XLA Modules:
  0.0 704.4 jit_solution(5128577823372429109)
XLA Ops:
  16.0 7.3 %all-to-all-start = ((bf16[8,128,1024]{2,1,0:T(8,128)(2,1)}), bf16[8,128,1024]{2,1,0:T(8,128)(2,1)S(1)}, u32[]{:S(2)}, u32[]{:S(2)}) async-start(bf16[8,128,1024]{2,1,0:T(8,128)(2,1)} %broadcast_select_fusion), calls=%async_computation | async-start | bytes 4194304 | tf_op jit(solution)/shard_map/all_to_all | solution.py:60
  23.8 47.7 %all-to-all-done = bf16[8,128,1024]{2,1,0:T(8,128)(2,1)S(1)} async-done(((bf16[8,128,1024]{2,1,0:T(8,128)(2,1)}), bf16[8,128,1024]{2,1,0:T(8,128)(2,1)S(1)}, u32[]{:S(2)}, u32[]{:S(2)}) %all-to-all-start) | async-done | bytes 2097184 | tf_op jit(solution)/shard_map/all_to_all | solution.py:60
  71.5 13.6 %pad_maximum_fusion = bf16[56,128,1024]{2,1,0:T(8,128)(2,1)} fusion(bf16[8,128,1024]{2,1,0:T(8,128)(2,1)S(1)} %all-to-all-done, bf16[48,128,1024]{2,1,0:T(8,128)(2,1)} %bitcast.134), kind=kLoop, calls=%fused_computation.5 | loop fusion | flops 7340032 | bytes 29360128 | tf_op jit(solution)/shard_map/concatenate | solution.py:67
  85.1 10.4 %gather_fusion.1 = bf16[32,128,1024]{2,1,0:T(8,128)(2,1)} fusion(bf16[56,128,1024]{2,1,0:T(8,128)(2,1)} %pad_maximum_fusion, s32[1024]{0:T(1024)S(1)} %pad_clamp_fusion), kind=kCustom, calls=%fused_computation.1 | custom fusion | bytes 16777344 | tf_op jit(solution)/shard_map/gather | solution.py:69
  95.4 15.6 %fusion.30 = f32[1024,1024]{0,1:T(8,128)} fusion(bf16[32,128,1024]{2,1,0:T(8,128)(2,1)} %gather_fusion.1, pred[32]{0:T(512)(128)(4,1)S(1)} %reduce_or.41), kind=kOutput, calls=%fused_computation.43 | convolution fusion | flops 8594128896 | bytes 12582944 | tf_op jit(solution)/shard_map/dot_general | solution.py:12
  111.2 11.6 %copy.26 = bf16[4096,1024]{0,1:T(8,128)(2,1)} copy(bf16[4096,1024]{1,0:T(8,128)(2,1)} %bitcast.132) | data formatting | bytes 16777216 | tf_op jit(solution)/shard_map/gather | solution.py:69
  122.7 11.5 %fusion.90 = (f32[1024,4096]{1,0:T(8,128)}, bf16[1024,4096]{1,0:T(8,128)(2,1)}) fusion(bf16[4096,1024]{0,1:T(8,128)(2,1)} %copy.26, pred[4096]{0:T(1024)(128)(4,1)S(1)} %broadcast_bitcast_fusion), kind=kLoop, calls=%fused_computation.208 | loop fusion | flops 8388608 | bytes 33558528 | tf_op jit(solution)/shard_map/transpose | solution.py:21
  134.3 118.5 %all-reduce.3.cloned.1.call-done = f32[1024,1024]{0,1:T(8,128)} async-done(((f32[1024,1024]{0,1:T(8,128)}), f32[1024,1024]{0,1:T(8,128)}) %all-reduce.3.cloned.1.call-update) | async-done | bytes 4194320 | tf_op jit(solution)/shard_map/psum | solution.py:15
  264.7 11.7 %cholesky.223 = f32[128,128]{1,0:T(8,128)S(1)} custom-call(f32[128,128]{1,0:T(8,128)S(1)} %cholesky.580), custom_call_target="Cholesky" | custom-call | tf_op jit(solution)/shard_map/jit(cholesky)/cholesky | solution.py:16
  277.1 9.8 %custom-call.63 = f32[1,128,128]{1,2,0:T(8,128)S(1)} custom-call(f32[1,128,128]{2,1,0:T(8,128)S(1)} %get-tuple-element.83), custom_call_target="InvertDiagBlocksLowerTriangular" | custom-call | tf_op jit(solution)/shard_map/jit(cholesky)/cholesky | solution.py:16
  293.4 12.2 %cholesky.244 = f32[128,128]{1,0:T(8,128)S(1)} custom-call(f32[128,128]{1,0:T(8,128)S(1)} %cholesky.584), custom_call_target="Cholesky" | custom-call | tf_op jit(solution)/shard_map/jit(cholesky)/cholesky | solution.py:16
  306.9 9.8 %custom-call.64 = f32[1,128,128]{1,2,0:T(8,128)S(1)} custom-call(f32[1,128,128]{2,1,0:T(8,128)S(1)} %get-tuple-element.80), custom_call_target="InvertDiagBlocksLowerTriangular" | custom-call | tf_op jit(solution)/shard_map/jit(cholesky)/cholesky | solution.py:16
  320.0 11.7 %cholesky.468 = f32[128,128]{1,0:T(8,128)S(1)} custom-call(f32[128,128]{1,0:T(8,128)S(1)} %cholesky.589), custom_call_target="Cholesky" | custom-call | tf_op jit(solution)/shard_map/jit(cholesky)/cholesky | solution.py:16
  333.0 9.8 %custom-call.65 = f32[1,128,128]{1,2,0:T(8,128)S(1)} custom-call(f32[1,128,128]{2,1,0:T(8,128)S(1)} %get-tuple-element.77), custom_call_target="InvertDiagBlocksLowerTriangular" | custom-call | tf_op jit(solution)/shard_map/jit(cholesky)/cholesky | solution.py:16
  346.3 11.8 %cholesky.487 = f32[128,128]{1,0:T(8,128)S(1)} custom-call(f32[128,128]{1,0:T(8,128)S(1)} %cholesky.594), custom_call_target="Cholesky" | custom-call | tf_op jit(solution)/shard_map/jit(cholesky)/cholesky | solution.py:16
  359.5 9.8 %custom-call.66 = f32[1,128,128]{1,2,0:T(8,128)S(1)} custom-call(f32[1,128,128]{2,1,0:T(8,128)S(1)} %get-tuple-element.74), custom_call_target="InvertDiagBlocksLowerTriangular" | custom-call | tf_op jit(solution)/shard_map/jit(cholesky)/cholesky | solution.py:16
  372.7 11.7 %cholesky.506 = f32[128,128]{1,0:T(8,128)S(1)} custom-call(f32[128,128]{1,0:T(8,128)S(1)} %cholesky.599), custom_call_target="Cholesky" | custom-call | tf_op jit(solution)/shard_map/jit(cholesky)/cholesky | solution.py:16
  385.8 10.0 %custom-call.67 = f32[1,128,128]{1,2,0:T(8,128)S(1)} custom-call(f32[1,128,128]{2,1,0:T(8,128)S(1)} %get-tuple-element.71), custom_call_target="InvertDiagBlocksLowerTriangular" | custom-call | tf_op jit(solution)/shard_map/jit(cholesky)/cholesky | solution.py:16
  399.0 11.7 %cholesky.526 = f32[128,128]{1,0:T(8,128)S(1)} custom-call(f32[128,128]{1,0:T(8,128)S(1)} %cholesky.604), custom_call_target="Cholesky" | custom-call | tf_op jit(solution)/shard_map/jit(cholesky)/cholesky | solution.py:16
  412.0 9.8 %custom-call.68 = f32[1,128,128]{1,2,0:T(8,128)S(1)} custom-call(f32[1,128,128]{2,1,0:T(8,128)S(1)} %get-tuple-element.68), custom_call_target="InvertDiagBlocksLowerTriangular" | custom-call | tf_op jit(solution)/shard_map/jit(cholesky)/cholesky | solution.py:16
  424.8 12.1 %cholesky.546 = f32[128,128]{1,0:T(8,128)S(1)} custom-call(f32[128,128]{1,0:T(8,128)S(1)} %cholesky.609), custom_call_target="Cholesky" | custom-call | tf_op jit(solution)/shard_map/jit(cholesky)/cholesky | solution.py:16
  438.2 9.8 %custom-call.69 = f32[1,128,128]{1,2,0:T(8,128)S(1)} custom-call(f32[1,128,128]{2,1,0:T(8,128)S(1)} %get-tuple-element.65), custom_call_target="InvertDiagBlocksLowerTriangular" | custom-call | tf_op jit(solution)/shard_map/jit(cholesky)/cholesky | solution.py:16
  450.7 11.7 %cholesky.564 = f32[128,128]{1,0:T(8,128)S(1)} custom-call(f32[128,128]{1,0:T(8,128)S(1)} %convolution_subtract_fusion.11), custom_call_target="Cholesky" | custom-call | tf_op jit(solution)/shard_map/jit(cholesky)/cholesky | solution.py:16
  468.6 6.7 multiply_bitcast_fusion
  480.7 23.4 %while.1 = (s32[]{:T(128)}, f32[1024,1024]{1,0:T(8,128)}, s32[8,2]{0,1:T(2,128)S(1)}, f32[8,128,128]{2,1,0:T(8,128)S(1)}, s32[]{:T(128)}) while((s32[]{:T(128)}, f32[1024,1024]{1,0:T(8,128)}, s32[8,2]{0,1:T(2,128)S(1)}, f32[8,128,128]{2,1,0:T(8,128)S(1)}, s32[]{:T(128)}) %tuple.74), condition=%wide.while_cond, body=%wide.while_body.sunk | while | flops 2 | bytes 131189 | solution.py:20
  504.1 78.8 %custom-call.70 = f32[8,128,128]{1,2,0:T(8,128)S(1)} custom-call(f32[8,128,128]{2,1,0:T(8,128)S(1)} %get-tuple-element.9), custom_call_target="InvertDiagBlocksLowerTriangular" | custom-call | tf_op jit(solution)/shard_map/jit(_solve_triangular)/triangular_solve | solution.py:20
  618.2 6.4 fusion.21
  630.9 9.3 %convolution_subtract_fusion.1 = f32[128,4096]{1,0:T(8,128)S(1)} fusion(f32[640,4096]{1,0:T(8,128)} %get-tuple-element.45, f32[1024,4096]{1,0:T(8,128)S(1)} %bitcast.131, f32[1024,1024]{1,0:T(8,128)} %get-tuple-element.145), kind=kOutput, calls=%fused_computation.27 | convolution fusion | flops 4027056128 | bytes 15007744 | tf_op jit(solution)/shard_map/jit(_solve_triangular)/triangular_solve | solution.py:20
  645.8 9.8 %convolution_subtract_fusion = f32[128,4096]{1,0:T(8,128)S(1)} fusion(f32[768,4096]{1,0:T(8,128)} %get-tuple-element.41, f32[1024,4096]{1,0:T(8,128)S(1)} %bitcast.131, f32[1024,1024]{1,0:T(8,128)} %get-tuple-element.145), kind=kOutput, calls=%fused_computation.26 | convolution fusion | flops 4832362496 | bytes 17170432 | tf_op jit(solution)/shard_map/jit(_solve_triangular)/triangular_solve | solution.py:20
  660.4 11.7 %convolution_subtract_fusion.4 = f32[128,4096]{1,0:T(8,128)S(1)} fusion(f32[896,4096]{1,0:T(8,128)} %get-tuple-element.37, f32[1024,4096]{1,0:T(8,128)S(1)} %bitcast.131, f32[1024,1024]{1,0:T(8,128)} %get-tuple-element.145), kind=kOutput, calls=%fused_computation.30 | convolution fusion | flops 5637668864 | bytes 19333120 | tf_op jit(solution)/shard_map/jit(_solve_triangular)/triangular_solve | solution.py:20
  676.2 9.2 %fusion = bf16[4096,1024]{0,1:T(8,128)(2,1)} fusion(f32[1024,4096]{1,0:T(8,128)} %convolution_dynamic-update-slice_fusion), kind=kLoop, calls=%fused_computation.6 | loop fusion | flops 8388608 | bytes 25165824 | tf_op jit(solution)/shard_map/convert_element_type | solution.py:23
  685.4 11.9 %copy.27 = bf16[4096,1024]{1,0:T(8,128)(2,1)} copy(bf16[4096,1024]{0,1:T(8,128)(2,1)} %fusion) | data formatting | bytes 16777216
  (113 shorter events, 141.2 us)
Async XLA Ops:
  16.0 55.5 %all-to-all-start = ((bf16[8,128,1024]{2,1,0:T(8,128)(2,1)}), bf16[8,128,1024]{2,1,0:T(8,128)(2,1)S(1)}, u32[]{:S(2)}, u32[]{:S(2)}) async-start(bf16[8,128,1024]{2,1,0:T(8,128)(2,1)} %broadcast_select_fusion), calls=%async_computation | async-start | bytes 4194304 | tf_op jit(solution)/shard_map/all_to_all | solution.py:60
  23.3 229.5 %all-reduce.3.cloned.1.call-start = ((), (), s32[]{:S(2)}) async-start(), calls=%async_computation.1 | async-start | bytes 8388608 | tf_op jit(solution)/shard_map/psum | solution.py:15
  262.8 1.9 copy-start
  582.9 29.7 %copy-start.1 = (f32[8,128,128]{1,2,0:T(8,128)}, f32[8,128,128]{1,2,0:T(8,128)S(1)}, u32[]{:S(2)}) copy-start(f32[8,128,128]{1,2,0:T(8,128)S(1)} %custom-call.70) | copy-start | bytes 1572868
  582.9 15.6 %slice-start = ((s8[16777216]{0:T(1024)(128)(4,1)}), s8[4194304]{0:T(1024)(128)(4,1)S(1)}, s32[]{:S(2)}) async-start(s8[16777216]{0:T(1024)(128)(4,1)} %bitcast.130), calls=%async_computation.2 | async-start | bytes 8388608
  582.9 15.6 %slice-start.1 = ((s8[16777216]{0:T(1024)(128)(4,1)}), s8[4194304]{0:T(1024)(128)(4,1)S(1)}, s32[]{:S(2)}) async-start(s8[16777216]{0:T(1024)(128)(4,1)} %bitcast.130), calls=%async_computation.3 | async-start | bytes 8388608
  589.0 9.5 %slice-start.2 = ((s8[16777216]{0:T(1024)(128)(4,1)}), s8[4194304]{0:T(1024)(128)(4,1)S(1)}, s32[]{:S(2)}) async-start(s8[16777216]{0:T(1024)(128)(4,1)} %bitcast.130), calls=%async_computation.4 | async-start | bytes 8388608
  592.8 5.8 slice-start.3
Sparse Core Ops, SparseCore 0:
  111.2 141.4 all-reduce.2
where the time goes:
time: 712 us; the launch traced here: 704 us
  other arithmetic  301 us (42%)
  waiting for transfers between devices  166 us (23%)
  matrix products  132 us (19%)
  local copies, waits for them, and re-layouts  78 us (11%)
  between operations  19.5 us (3%)
  starting transfers between devices  7.32 us (1%)
    another operation x31, other arithmetic, factor(): return jnp.linalg.cholesky(summed)  173 us
    psum x1, waiting for transfers between devices, factor(): summed = lax.psum(gram_local, ('gx', 'gy'))  118 us
    another operation x15, matrix products, normalise(): jax.scipy.linalg.solve_triangular(low_factor, row_block.astype(jnp.float3...  93.2 us
    another operation x2, other arithmetic, normalise(): jax.scipy.linalg.solve_triangular(low_factor, row_block.astype(jnp.float3...  78.8 us
    all_to_all x1, waiting for transfers between devices, on_device(): lax.all_to_all(jnp.where(send_has[:, None, None], tile_stack[send_index],...  47.7 us
    another operation x24, local copies, waits for them, and re-layouts  23.3 us
    another operation x14, matrix products, factor(): return jnp.linalg.cholesky(summed)  23 us
    gather x2, local copies, waits for them, and re-layouts, on_device(): combined[source]  21.9 us
  transfers between devices with their start and end apart: 2, of which 2 were waited for; matrix products, arithmetic and copies ran while one was open for 3% of the time, Pallas kernels for 0%

commit v1 on v0

--- a/solution.py
+++ b/solution.py
@@ -12,7 +12,7 @@
     gram_local = lax.dot_general(
         row_block, row_block, (((0,), (0,)), ((), ())), preferred_element_type=jnp.float32
     )
-    summed = lax.psum(gram_local, ("gx", "gy"))
+    summed = lax.psum(lax.psum(gram_local, "gy"), "gx")
     return jnp.linalg.cholesky(summed)
 
 

time: 712 us -> 813 us (1.14)
  waiting for transfers between devices: 166 us -> 267 us
    psum x1 -> x2, waiting for transfers between devices: 118 us -> 219 us  [factor(): summed = lax.psum(lax.psum(gram_local, 'gy'), 'gx')]
  transfers between devices with their start and end apart: 2 -> 3, of which waited for: 2 -> 3; matrix products, arithmetic and copies ran while one was open for 3% -> 3% of each run, Pallas kernels for 0% -> 0%
where the time goes in v1:
time: 813 us; the launch traced here: 805 us
  other arithmetic  301 us (37%)
  waiting for transfers between devices  267 us (33%)
  matrix products  132 us (16%)
  local copies, waits for them, and re-layouts  77.8 us (10%)
  between operations  19.5 us (2%)
    psum x2, waiting for transfers between devices, factor(): summed = lax.psum(lax.psum(gram_local, 'gy'), 'gx')  219 us
    another operation x31, other arithmetic, factor(): return jnp.linalg.cholesky(summed)  173 us
    another operation x15, matrix products, normalise(): jax.scipy.linalg.solve_triangular(low_factor, row_block.astype(jnp.float3...  93.2 us
    another operation x2, other arithmetic, normalise(): jax.scipy.linalg.solve_triangular(low_factor, row_block.astype(jnp.float3...  78.8 us
    all_to_all x1, waiting for transfers between devices, on_device(): lax.all_to_all(jnp.where(send_has[:, None, None], tile_stack[send_index],...  47.7 us
    another operation x24, local copies, waits for them, and re-layouts  23.3 us
    another operation x14, matrix products, factor(): return jnp.linalg.cholesky(summed)  23 us
    gather x2, local copies, waits for them, and re-layouts, on_device(): combined[source]  21.7 us
  transfers between devices with their start and end apart: 3, of which 3 were waited for; matrix products, arithmetic and copies ran while one was open for 3% of the time, Pallas kernels for 0%

profile of v1, /device:TPU:0, one launch (start us, length us, event | category | flops | bytes accessed | tf_op | source)
XLA Modules:
  0.0 805.1 jit_solution(15092592858500640551)
XLA Ops:
  16.0 7.3 all-to-all-start
  23.8 47.7 %all-to-all-done = bf16[8,128,1024]{2,1,0:T(8,128)(2,1)S(1)} async-done(((bf16[8,128,1024]{2,1,0:T(8,128)(2,1)}), bf16[8,128,1024]{2,1,0:T(8,128)(2,1)S(1)}, u32[]{:S(2)}, u32[]{:S(2)}) %all-to-all-start) | async-done | bytes 2097184 | tf_op jit(solution)/shard_map/all_to_all | solution.py:60
  71.5 13.6 %pad_maximum_fusion = bf16[56,128,1024]{2,1,0:T(8,128)(2,1)} fusion(bf16[8,128,1024]{2,1,0:T(8,128)(2,1)S(1)} %all-to-all-done, bf16[48,128,1024]{2,1,0:T(8,128)(2,1)} %bitcast.134), kind=kLoop, calls=%fused_computation.5 | loop fusion | flops 7340032 | bytes 29360128 | tf_op jit(solution)/shard_map/concatenate | solution.py:67
  85.1 10.4 %gather_fusion.1 = bf16[32,128,1024]{2,1,0:T(8,128)(2,1)} fusion(bf16[56,128,1024]{2,1,0:T(8,128)(2,1)} %pad_maximum_fusion, s32[1024]{0:T(1024)S(1)} %pad_clamp_fusion), kind=kCustom, calls=%fused_computation.1 | custom fusion | bytes 16777344 | tf_op jit(solution)/shard_map/gather | solution.py:69
  95.4 15.6 %fusion.30 = f32[1024,1024]{0,1:T(8,128)} fusion(bf16[32,128,1024]{2,1,0:T(8,128)(2,1)} %gather_fusion.1, pred[32]{0:T(512)(128)(4,1)S(1)} %reduce_or.41), kind=kOutput, calls=%fused_computation.43 | convolution fusion | flops 8594128896 | bytes 12582944 | tf_op jit(solution)/shard_map/dot_general | solution.py:12
  111.1 155.5 %all-reduce.4.cloned.1.call-done = f32[1024,1024]{0,1:T(8,128)} async-done(((f32[1024,1024]{0,1:T(8,128)}), f32[1024,1024]{0,1:T(8,128)}) %all-reduce.4.cloned.1.call-update) | async-done | bytes 4194320 | tf_op jit(solution)/shard_map/psum | solution.py:15
  266.7 11.3 %copy.26 = bf16[4096,1024]{0,1:T(8,128)(2,1)} copy(bf16[4096,1024]{1,0:T(8,128)(2,1)} %bitcast.132) | data formatting | bytes 16777216 | tf_op jit(solution)/shard_map/gather | solution.py:69
  278.0 11.5 %fusion.90 = (f32[1024,4096]{1,0:T(8,128)}, bf16[1024,4096]{1,0:T(8,128)(2,1)}) fusion(bf16[4096,1024]{0,1:T(8,128)(2,1)} %copy.26, pred[4096]{0:T(1024)(128)(4,1)S(1)} %broadcast_bitcast_fusion), kind=kLoop, calls=%fused_computation.208 | loop fusion | flops 8388608 | bytes 33558528 | tf_op jit(solution)/shard_map/transpose | solution.py:21
  289.6 63.9 %all-reduce.6.cloned.1.call-done = f32[1024,1024]{0,1:T(8,128)} async-done(((f32[1024,1024]{0,1:T(8,128)}), f32[1024,1024]{0,1:T(8,128)}) %all-reduce.6.cloned.1.call-update) | async-done | bytes 4194320 | tf_op jit(solution)/shard_map/psum | solution.py:15
  365.5 11.7 %cholesky.223 = f32[128,128]{1,0:T(8,128)S(1)} custom-call(f32[128,128]{1,0:T(8,128)S(1)} %cholesky.580), custom_call_target="Cholesky" | custom-call | tf_op jit(solution)/shard_map/jit(cholesky)/cholesky | solution.py:16
  377.9 9.8 %custom-call.63 = f32[1,128,128]{1,2,0:T(8,128)S(1)} custom-call(f32[1,128,128]{2,1,0:T(8,128)S(1)} %get-tuple-element.83), custom_call_target="InvertDiagBlocksLowerTriangular" | custom-call | tf_op jit(solution)/shard_map/jit(cholesky)/cholesky | solution.py:16
  394.1 12.2 %cholesky.244 = f32[128,128]{1,0:T(8,128)S(1)} custom-call(f32[128,128]{1,0:T(8,128)S(1)} %cholesky.584), custom_call_target="Cholesky" | custom-call | tf_op jit(solution)/shard_map/jit(cholesky)/cholesky | solution.py:16
  407.6 9.8 %custom-call.64 = f32[1,128,128]{1,2,0:T(8,128)S(1)} custom-call(f32[1,128,128]{2,1,0:T(8,128)S(1)} %get-tuple-element.80), custom_call_target="InvertDiagBlocksLowerTriangular" | custom-call | tf_op jit(solution)/shard_map/jit(cholesky)/cholesky | solution.py:16
  420.7 11.7 %cholesky.468 = f32[128,128]{1,0:T(8,128)S(1)} custom-call(f32[128,128]{1,0:T(8,128)S(1)} %cholesky.589), custom_call_target="Cholesky" | custom-call | tf_op jit(solution)/shard_map/jit(cholesky)/cholesky | solution.py:16
  433.7 9.8 %custom-call.65 = f32[1,128,128]{1,2,0:T(8,128)S(1)} custom-call(f32[1,128,128]{2,1,0:T(8,128)S(1)} %get-tuple-element.77), custom_call_target="InvertDiagBlocksLowerTriangular" | custom-call | tf_op jit(solution)/shard_map/jit(cholesky)/cholesky | solution.py:16
  447.0 11.8 %cholesky.487 = f32[128,128]{1,0:T(8,128)S(1)} custom-call(f32[128,128]{1,0:T(8,128)S(1)} %cholesky.594), custom_call_target="Cholesky" | custom-call | tf_op jit(solution)/shard_map/jit(cholesky)/cholesky | solution.py:16
  460.2 9.8 %custom-call.66 = f32[1,128,128]{1,2,0:T(8,128)S(1)} custom-call(f32[1,128,128]{2,1,0:T(8,128)S(1)} %get-tuple-element.74), custom_call_target="InvertDiagBlocksLowerTriangular" | custom-call | tf_op jit(solution)/shard_map/jit(cholesky)/cholesky | solution.py:16
  473.5 11.7 %cholesky.506 = f32[128,128]{1,0:T(8,128)S(1)} custom-call(f32[128,128]{1,0:T(8,128)S(1)} %cholesky.599), custom_call_target="Cholesky" | custom-call | tf_op jit(solution)/shard_map/jit(cholesky)/cholesky | solution.py:16
  486.5 10.0 %custom-call.67 = f32[1,128,128]{1,2,0:T(8,128)S(1)} custom-call(f32[1,128,128]{2,1,0:T(8,128)S(1)} %get-tuple-element.71), custom_call_target="InvertDiagBlocksLowerTriangular" | custom-call | tf_op jit(solution)/shard_map/jit(cholesky)/cholesky | solution.py:16
  499.8 11.7 %cholesky.526 = f32[128,128]{1,0:T(8,128)S(1)} custom-call(f32[128,128]{1,0:T(8,128)S(1)} %cholesky.604), custom_call_target="Cholesky" | custom-call | tf_op jit(solution)/shard_map/jit(cholesky)/cholesky | solution.py:16
  512.7 9.8 %custom-call.68 = f32[1,128,128]{1,2,0:T(8,128)S(1)} custom-call(f32[1,128,128]{2,1,0:T(8,128)S(1)} %get-tuple-element.68), custom_call_target="InvertDiagBlocksLowerTriangular" | custom-call | tf_op jit(solution)/shard_map/jit(cholesky)/cholesky | solution.py:16
  525.6 12.1 %cholesky.546 = f32[128,128]{1,0:T(8,128)S(1)} custom-call(f32[128,128]{1,0:T(8,128)S(1)} %cholesky.609), custom_call_target="Cholesky" | custom-call | tf_op jit(solution)/shard_map/jit(cholesky)/cholesky | solution.py:16
  539.0 9.8 %custom-call.69 = f32[1,128,128]{1,2,0:T(8,128)S(1)} custom-call(f32[1,128,128]{2,1,0:T(8,128)S(1)} %get-tuple-element.65), custom_call_target="InvertDiagBlocksLowerTriangular" | custom-call | tf_op jit(solution)/shard_map/jit(cholesky)/cholesky | solution.py:16
  551.5 11.7 %cholesky.564 = f32[128,128]{1,0:T(8,128)S(1)} custom-call(f32[128,128]{1,0:T(8,128)S(1)} %convolution_subtract_fusion.11), custom_call_target="Cholesky" | custom-call | tf_op jit(solution)/shard_map/jit(cholesky)/cholesky | solution.py:16
  569.4 6.7 multiply_bitcast_fusion
  581.4 23.4 %while.1 = (s32[]{:T(128)}, f32[1024,1024]{1,0:T(8,128)}, s32[8,2]{0,1:T(2,128)S(1)}, f32[8,128,128]{2,1,0:T(8,128)S(1)}, s32[]{:T(128)}) while((s32[]{:T(128)}, f32[1024,1024]{1,0:T(8,128)}, s32[8,2]{0,1:T(2,128)S(1)}, f32[8,128,128]{2,1,0:T(8,128)S(1)}, s32[]{:T(128)}) %tuple.74), condition=%wide.while_cond, body=%wide.while_body.sunk | while | flops 2 | bytes 131189 | solution.py:20
  604.8 78.8 %custom-call.70 = f32[8,128,128]{1,2,0:T(8,128)S(1)} custom-call(f32[8,128,128]{2,1,0:T(8,128)S(1)} %get-tuple-element.9), custom_call_target="InvertDiagBlocksLowerTriangular" | custom-call | tf_op jit(solution)/shard_map/jit(_solve_triangular)/triangular_solve | solution.py:20
  731.6 9.3 %convolution_subtract_fusion.1 = f32[128,4096]{1,0:T(8,128)S(1)} fusion(f32[640,4096]{1,0:T(8,128)} %get-tuple-element.45, f32[1024,4096]{1,0:T(8,128)S(1)} %bitcast.131, f32[1024,1024]{1,0:T(8,128)} %get-tuple-element.146), kind=kOutput, calls=%fused_computation.27 | convolution fusion | flops 4027056128 | bytes 15007744 | tf_op jit(solution)/shard_map/jit(_solve_triangular)/triangular_solve | solution.py:20
  746.5 9.8 %convolution_subtract_fusion = f32[128,4096]{1,0:T(8,128)S(1)} fusion(f32[768,4096]{1,0:T(8,128)} %get-tuple-element.41, f32[1024,4096]{1,0:T(8,128)S(1)} %bitcast.131, f32[1024,1024]{1,0:T(8,128)} %get-tuple-element.146), kind=kOutput, calls=%fused_computation.26 | convolution fusion | flops 4832362496 | bytes 17170432 | tf_op jit(solution)/shard_map/jit(_solve_triangular)/triangular_solve | solution.py:20
  761.1 11.7 %convolution_subtract_fusion.4 = f32[128,4096]{1,0:T(8,128)S(1)} fusion(f32[896,4096]{1,0:T(8,128)} %get-tuple-element.37, f32[1024,4096]{1,0:T(8,128)S(1)} %bitcast.131, f32[1024,1024]{1,0:T(8,128)} %get-tuple-element.146), kind=kOutput, calls=%fused_computation.30 | convolution fusion | flops 5637668864 | bytes 19333120 | tf_op jit(solution)/shard_map/jit(_solve_triangular)/triangular_solve | solution.py:20
  777.0 9.2 %fusion = bf16[4096,1024]{0,1:T(8,128)(2,1)} fusion(f32[1024,4096]{1,0:T(8,128)} %convolution_dynamic-update-slice_fusion), kind=kLoop, calls=%fused_computation.6 | loop fusion | flops 8388608 | bytes 25165824 | tf_op jit(solution)/shard_map/convert_element_type | solution.py:23
  786.2 11.9 %copy.27 = bf16[4096,1024]{1,0:T(8,128)(2,1)} copy(bf16[4096,1024]{0,1:T(8,128)(2,1)} %fusion) | data formatting | bytes 16777216
  (116 shorter events, 147.7 us)
Async XLA Ops:
  16.0 55.5 %all-to-all-start = ((bf16[8,128,1024]{2,1,0:T(8,128)(2,1)}), bf16[8,128,1024]{2,1,0:T(8,128)(2,1)S(1)}, u32[]{:S(2)}, u32[]{:S(2)}) async-start(bf16[8,128,1024]{2,1,0:T(8,128)(2,1)} %broadcast_select_fusion), calls=%async_computation | async-start | bytes 4194304 | tf_op jit(solution)/shard_map/all_to_all | solution.py:60
  23.3 243.3 %all-reduce.4.cloned.1.call-start = ((), (), s32[]{:S(2)}) async-start(), calls=%async_computation.1 | async-start | bytes 8388608 | tf_op jit(solution)/shard_map/psum | solution.py:15
  111.1 242.4 %all-reduce.6.cloned.1.call-start = ((), (), s32[]{:S(2)}) async-start(), calls=%async_computation.2 | async-start | bytes 8388608 | tf_op jit(solution)/shard_map/psum | solution.py:15
  363.5 1.9 copy-start
  683.6 29.7 %copy-start.1 = (f32[8,128,128]{1,2,0:T(8,128)}, f32[8,128,128]{1,2,0:T(8,128)S(1)}, u32[]{:S(2)}) copy-start(f32[8,128,128]{1,2,0:T(8,128)S(1)} %custom-call.70) | copy-start | bytes 1572868
  683.6 15.6 %slice-start = ((s8[16777216]{0:T(1024)(128)(4,1)}), s8[4194304]{0:T(1024)(128)(4,1)S(1)}, s32[]{:S(2)}) async-start(s8[16777216]{0:T(1024)(128)(4,1)} %bitcast.130), calls=%async_computation.3 | async-start | bytes 8388608
  683.6 15.6 %slice-start.1 = ((s8[16777216]{0:T(1024)(128)(4,1)}), s8[4194304]{0:T(1024)(128)(4,1)S(1)}, s32[]{:S(2)}) async-start(s8[16777216]{0:T(1024)(128)(4,1)} %bitcast.130), calls=%async_computation.4 | async-start | bytes 8388608
  689.7 9.5 %slice-start.2 = ((s8[16777216]{0:T(1024)(128)(4,1)}), s8[4194304]{0:T(1024)(128)(4,1)S(1)}, s32[]{:S(2)}) async-start(s8[16777216]{0:T(1024)(128)(4,1)} %bitcast.130), calls=%async_computation.5 | async-start | bytes 8388608
  693.5 5.8 slice-start.3
Sparse Core Ops, SparseCore 0:
  111.2 155.3 all-reduce.3
  269.0 84.4 all-reduce.5
